TPU v7x, 32 devices: a whole 2x2x4 slice. The times are simulated.
32 devices in a mesh: box: 16 (over z, x, core), shift: 2 (over y).
Axes of the slice: x: 2, y: 2, z: 4, core: 2. Of those that a mesh axis runs over, the one named last changes fastest.
Arguments:
- vectors: bfloat16 [2, 1024, 128, 128], P('shift', 'box'), may hold values from -6 to 6
- sigma: float32 [2, 2], P('shift'), may hold values from 0.5 to 2
- near_blocks: bfloat16 [1024, 6, 128, 128], P('box', None, 'shift'), may hold values from -0.21875 to 0.21875
- near_index: int32 [1024, 6], P('box'), may hold values from -1 to 1023, as said below
- radiate: bfloat16 [128, 128], replicated, may hold values from -0.5 to 0.5
- interp_one: bfloat16 [8, 512, 128], replicated, may hold values from -0.1875 to 0.1875
- interp_two: bfloat16 [8, 2048, 512], replicated, may hold values from -0.09375 to 0.09375
- trans_one: float32 [316, 512], replicated, may hold values from -1.5 to 1.5
- level1_source: int32 [128, 16], P('box'), may hold values from -1 to 127, as said below
- level1_offset: int32 [128, 16], P('box'), may hold values from 0 to 315
- trans_two: float32 [316, 2048], P(None, 'box'), may hold values from -1 to 1
- level2_source: int32 [16, 32], replicated, may hold values from -1 to 15, as said below
- level2_offset: int32 [16, 32], replicated, may hold values from 0 to 315
Outputs:
- applied: float32 [2, 1024, 128, 128], P('shift', 'box')
Inputs may be any that keep to these rules, and one draw needn't show every extreme that they name: `near_index`: leaf boxes are numbered along a space-filling curve. Entry 0 of each row is the box itself; every live entry names a box within 64 of the row's box; live entries come first, unused ones are -1; some rows use all 6 entries and some only one. `level1_source`: entry 0 of each row is live; every live entry names a box within 8 of the row's box; live entries come first, unused ones are -1; some rows use all 16 entries and some only one. `level2_source`: entry 0 of each row is live; live entries come first, unused ones are -1; some rows use all 32 entries and some only one.
All inputs are finite; a program needn't handle non-finite values.
Results may differ from a plain program's by a relative error of at most 0.0035.
Values may be sent and summed in bfloat16 or wider, within the bound.
No kernel may reach another device: no remote copies, remote signals or barrier semaphores. Data moves between devices by JAX's collectives and lax.ppermute only.
A program may use at most 192 MiB of HBM per device.

v0:
```python
import jax
import jax.numpy as jnp
from jax import lax
from jax.sharding import PartitionSpec as P


def extended(block, sides, width):
    for axis, dim in sides:
        count = lax.axis_size(axis)
        forward = [(i, i + 1) for i in range(count - 1)]
        backward = [(target, source) for source, target in forward]
        low = lax.ppermute(
            lax.slice_in_dim(block, block.shape[dim] - width, None, axis=dim), axis, forward
        )
        high = lax.ppermute(lax.slice_in_dim(block, 0, width, axis=dim), axis, backward)
        block = jnp.concatenate([low, block, high], axis=dim)
    return block


def weighted_lists(pattern, table, offsets, sources, base):
    live = sources >= 0
    local = jnp.where(live, sources - base, 0)
    weights = table[offsets] * live[:, :, None].astype(jnp.float32)
    picked = pattern[local]
    return jnp.einsum("cjk,cjkr->ckr", weights, picked, preferred_element_type=jnp.float32)


def body(
    vectors,
    sigma,
    near_blocks,
    near_index,
    radiate,
    interp_one,
    interp_two,
    trans_one,
    level1_source,
    level1_offset,
    trans_two,
    level2_source,
    level2_offset,
):
    box_count = vectors.shape[1]
    unknowns = vectors.shape[2]
    columns = vectors.shape[3]
    samples0 = radiate.shape[0]
    samples1 = interp_one.shape[1]
    my_box = lax.axis_index("box")
    live = near_index >= 0
    local = jnp.where(live, near_index - (my_box * box_count - box_count), 0)
    live_mask = live[:, :, None, None].astype(jnp.bfloat16)
    haloed = extended(vectors, (("box", 1),), box_count)[0]
    near_source = haloed[local] * live_mask
    near = jnp.einsum(
        "bjvu,bjur->bvr",
        lax.all_gather(near_blocks, "shift", axis=2, tiled=True),
        near_source,
        preferred_element_type=jnp.float32,
    )
    field = vectors[0]
    leaf = jnp.einsum("ku,bur->bkr", radiate, field, preferred_element_type=jnp.float32).astype(
        jnp.bfloat16
    )
    upper = jnp.einsum(
        "oqk,cokr->cqr",
        interp_one,
        leaf.reshape(box_count // 8, 8, samples0, columns),
        preferred_element_type=jnp.float32,
    ).astype(jnp.bfloat16)
    coarse = jnp.einsum(
        "oqk,gokr->gqr",
        interp_two,
        upper.reshape(box_count // 64, 8, samples1, columns),
        preferred_element_type=jnp.float32,
    ).astype(jnp.bfloat16)
    turned = weighted_lists(
        lax.all_to_all(coarse, "box", split_axis=1, concat_axis=0, tiled=True),
        trans_two,
        level2_offset,
        level2_source,
        0,
    ).astype(jnp.bfloat16)
    incoming = lax.all_to_all(turned, "box", split_axis=0, concat_axis=1, tiled=True)
    parents = box_count // 8
    upper_rim = extended(upper, (("box", 0),), parents)
    across = weighted_lists(
        upper_rim, trans_one, level1_offset, level1_source, my_box * parents - parents
    )
    down = jnp.einsum(
        "oqk,gqr->gokr", interp_two, incoming, preferred_element_type=jnp.float32
    ).reshape(parents, samples1, columns)
    local_in = (across + down).astype(jnp.bfloat16)
    leaf_in = (
        jnp.einsum("oqk,cqr->cokr", interp_one, local_in, preferred_element_type=jnp.float32)
        .reshape(box_count, samples0, columns)
        .astype(jnp.bfloat16)
    )
    far = jnp.einsum("ku,bkr->bur", radiate, leaf_in, preferred_element_type=jnp.float32)
    real_part = field[:, : unknowns // 2].astype(jnp.float32)
    imag_part = field[:, unknowns // 2 :].astype(jnp.float32)
    sig_re = sigma[0, 0]
    sig_im = sigma[0, 1]
    scaled = jnp.concatenate(
        [sig_re * real_part - sig_im * imag_part, sig_re * imag_part + sig_im * real_part], axis=1
    )
    return (near + far - scaled)[None]


def solution(mesh):
    in_specs = (
        P("shift", "box", None, None),
        P("shift", None),
        P("box", None, "shift", None),
        P("box", None),
        P(),
        P(),
        P(),
        P(),
        P("box", None),
        P("box", None),
        P(None, "box"),
        P(),
        P(),
    )
    out_specs = P("shift", "box", None, None)
    return jax.shard_map(body, mesh=mesh, in_specs=in_specs, out_specs=out_specs, check_vma=False)
```

profile of v0, /device:TPU:0, one launch (start us, length us, event | category | flops | bytes accessed | tf_op | source)
XLA Modules:
  0.0 232.8 jit_solution(10471339703910101869)
XLA Ops:
  7.4 2.3 %fusion.13 = bf16[64,128,128]{2,1,0:T(8,128)(2,1)S(1)} fusion(bf16[1,64,128,128]{3,2,1,0:T(8,128)(2,1)} %param.13, bf16[128,128]{1,0:T(8,128)(2,1)S(1)} %copy-done.5), kind=kOutput, calls=%fused_computation.29 | convolution fusion | flops 269484032 | bytes 4227072 | tf_op jit(solution)/shard_map/ku,bur->bkr/dot_general | solution.py:61
  9.7 2.3 fusion.16
  12.0 3.4 %collective-permute-start.2 = (bf16[8,512,128]{1,2,0:T(8,128)(2,1)}, bf16[8,512,128]{1,2,0:T(8,128)(2,1)}, u32[]{:S(2)}, u32[]{:S(2)}) collective-permute-start(bf16[8,512,128]{1,2,0:T(8,128)(2,1)} %fusion.16), channel_id=1, source_target_pairs={{0,2},{2,4},{4,6},{6,8},{8,10},{10,12},{12,14},{14,16},{16,18},{18... | collective-permute-start | bytes 3145736 | tf_op jit(solution)/shard_map/ppermute | solution.py:12
  15.4 1.3 collective-permute-start.3
  16.7 5.6 %collective-permute-start = (bf16[1,64,128,128]{3,2,1,0:T(8,128)(2,1)}, bf16[1,64,128,128]{3,2,1,0:T(8,128)(2,1)}, u32[]{:S(2)}, u32[]{:S(2)}) collective-permute-start(bf16[1,64,128,128]{3,2,1,0:T(8,128)(2,1)} %param.13), channel_id=1, source_target_pairs={{0,2},{2,4},{4,6},{6,8},{8,10},{10,12},{12,14},{14,16},{16,18},{18... | collective-permute-start | bytes 6291464 | tf_op jit(solution)/shard_map/ppermute | solution.py:12
  22.3 1.3 collective-permute-start.1
  23.6 13.4 %fusion.7 = bf16[1,2048,128]{1,2,0:T(8,128)(2,1)S(1)} fusion(bf16[8,512,128]{1,2,0:T(8,128)(2,1)} %fusion.16, bf16[8,2048,512]{2,1,0:T(8,128)(2,1)} %param.19), kind=kOutput, calls=%fused_computation.23 | convolution fusion | flops 2147745792 | bytes 18350080 | tf_op jit(solution)/shard_map/oqk,gokr->gqr/dot_general | solution.py:70
  38.3 11.5 %reduce.4 = bf16[2048,128]{1,0:T(8,128)(2,1)S(1)} reduce(bf16[2048,1,128]{2,1,0:T(2,128)(2,1)S(1)} %bitcast.102, bf16[]{:T(256)} %broadcast.53), dimensions={1}, to_apply=%bitcast.88.reduce_sub_computation | reduce | bytes 1048578
  50.8 7.6 %all-to-all-start = ((bf16[16,2,8192]{2,1,0:T(2,128)(2,1)}), bf16[16,2,8192]{2,1,0:T(2,128)(2,1)}, u32[]{:S(2)}, u32[]{:S(2)}) async-start(bf16[16,2,8192]{2,1,0:T(2,128)(2,1)} %reshape.95), calls=%async_computation | async-start | bytes 1048576 | tf_op jit(solution)/shard_map/all_to_all | solution.py:77
  59.7 3.2 %copy.34 = bf16[1,64,128,128]{2,3,1,0:T(8,128)(2,1)S(1)} copy(bf16[1,64,128,128]{3,2,1,0:T(8,128)(2,1)} %param.13) | data formatting | bytes 4194304 | tf_op args[0]
  63.1 2.7 %gather_fusion.1 = f32[128,512]{1,0:T(8,128)} fusion(f32[316,512]{1,0:T(8,128)} %param.20, s32[1024]{0:T(1024)S(1)} %pad_clamp_fusion.3), kind=kCustom, calls=%fused_computation.1 | custom fusion | bytes 524800 | tf_op jit(solution)/shard_map/gather | solution.py:23
  65.7 1.6 gather_fusion.3
  67.4 1.7 multiply_bitcast_fusion.1
  69.1 1.8 multiply_bitcast_fusion
  70.9 6.1 %fusion.3 = (f32[64,64,128]{1,2,0:T(8,128)}, f32[64,64,128]{1,2,0:T(8,128)}) fusion(f32[]{:T(128)} %bitcast.34, f32[]{:T(128)} %bitcast.33, bf16[64,128,128]{1,2,0:T(8,128)(2,1)S(1)} %bitcast.99), kind=kLoop, calls=%fused_computation.15 | loop fusion | flops 4194304 | bytes 6291464 | tf_op jit(solution)/shard_map/sub | solution.py:104
  77.0 2.2 reshape.96
  79.3 13.6 %gather_fusion.4 = bf16[512,128,128]{2,1,0:T(8,128)(2,1)} fusion(bf16[16,128,128]{2,1,0:T(8,128)(2,1)S(1)} %bitcast.97, s32[1024]{0:T(1024)S(1)} %pad_clamp_fusion), kind=kCustom, calls=%fused_computation.4 | custom fusion | bytes 33556480 | tf_op jit(solution)/shard_map/gather | solution.py:24
  93.0 11.4 %multiply_reduce_fusion = bf16[16,128,128]{2,1,0:T(8,128)(2,1)S(1)} fusion(f32[16,128,32]{1,2,0:T(8,128)S(1)} %copy-done.4, bf16[512,128,128]{2,1,0:T(8,128)(2,1)} %gather_fusion.4), kind=kLoop, calls=%fused_computation.5 | loop fusion | flops 24903680 | bytes 17563648
  104.4 1.0 copy.54
  105.4 20.4 %all-to-all-start.1 = ((bf16[16,128,128]{1,2,0:T(8,128)(2,1)}), bf16[16,128,128]{1,2,0:T(8,128)(2,1)}, u32[]{:S(2)}, u32[]{:S(2)}) async-start(bf16[16,128,128]{1,2,0:T(8,128)(2,1)} %copy.54), calls=%async_computation.1 | async-start | bytes 1048576 | tf_op jit(solution)/shard_map/all_to_all | solution.py:83
  125.8 3.3 %pad_maximum_fusion = bf16[24,512,128]{1,2,0:T(8,128)(2,1)} fusion(bf16[8,512,128]{1,2,0:T(8,128)(2,1)} %collective-permute-done.3, bf16[8,512,128]{1,2,0:T(8,128)(2,1)} %fusion.16, bf16[8,512,128]{1,2,0:T(8,128)(2,1)} %collective-permute-done.2), kind=kLoop, calls=%fused_computation.20 | loop fusion | flops 3145728 | bytes 6291456 | tf_op jit(solution)/shard_map/concatenate | solution.py:16
  129.0 10.1 %gather_fusion.2 = bf16[128,512,128]{1,2,0:T(8,128)(2,1)} fusion(bf16[24,512,128]{1,2,0:T(8,128)(2,1)} %pad_maximum_fusion, s32[1024]{0:T(1024)S(1)} %pad_clamp_fusion.2), kind=kCustom, calls=%fused_computation.2 | custom fusion | bytes 33554944 | tf_op jit(solution)/shard_map/gather | solution.py:24
  139.1 9.3 %multiply_reduce_fusion.1 = f32[8,512,128]{1,2,0:T(8,128)S(1)} fusion(f32[8,512,16]{1,2,0:T(8,128)S(1)} %copy-done.3, bf16[128,512,128]{1,2,0:T(8,128)(2,1)} %gather_fusion.2), kind=kLoop, calls=%fused_computation.6 | loop fusion | flops 24641536 | bytes 19136512 | tf_op jit(solution)/shard_map/cjk,cjkr->ckr/dot_general | solution.py:25
  148.4 2.2 copy.36
  150.6 2.1 reshape.92
  152.7 10.8 %convolution_convert_fusion = bf16[8,128,8,128]{3,1,2,0:T(8,128)(2,1)} fusion(bf16[8,512,128]{2,1,0:T(8,128)(2,1)S(1)} %copy-done, f32[8,512,128]{1,2,0:T(8,128)S(1)} %multiply_reduce_fusion.1, bf16[2048,128,1]{0,1,2:T(8,128)(2,1)} %reshape.92, bf16[8,2048,512]{2,1,0:T(8,128)(2,1)} %param.19), kind=kOutput, calls=%fused_computation.30 | convolution fusion | flops 3223322624 | bytes 22544384 | tf_op jit(solution)/shard_map/oqk,cqr->cokr/dot_general | solution.py:94
  163.4 4.2 %fusion.20 = f32[64,128,128]{2,1,0:T(8,128)} fusion(bf16[64,128,128]{1,2,0:T(8,128)(2,1)} %bitcast.100, bf16[128,128]{1,0:T(8,128)(2,1)S(1)} %copy-done.5), kind=kOutput, calls=%fused_computation.37 | convolution fusion | flops 268435456 | bytes 6324224 | tf_op jit(solution)/shard_map/ku,bkr->bur/dot_general | solution.py:98
  167.7 6.0 %maximum_bitcast_fusion = bf16[192,128,128]{2,1,0:T(8,128)(2,1)} fusion(bf16[1,64,128,128]{3,2,1,0:T(8,128)(2,1)} %collective-permute-done.1, bf16[1,64,128,128]{3,2,1,0:T(8,128)(2,1)} %param.13, bf16[1,64,128,128]{3,2,1,0:T(8,128)(2,1)} %collective-permute-done), kind=kLoop, calls=%fused_computation.9 | loop fusion | flops 6291456 | bytes 12582912 | tf_op jit(solution)/shard_map/squeeze | solution.py:52
  173.7 13.9 %gather_fusion = bf16[384,128,128]{2,1,0:T(8,128)(2,1)} fusion(bf16[192,128,128]{2,1,0:T(8,128)(2,1)} %maximum_bitcast_fusion, s32[1024]{0:T(1024)S(1)} %pad_clamp_fusion.4), kind=kCustom, calls=%fused_computation | custom fusion | bytes 25167360 | tf_op jit(solution)/shard_map/gather | solution.py:53
  187.6 16.6 %copy.33 = bf16[64,6,128,128]{2,3,1,0:T(8,128)(2,1)} copy(bf16[64,6,128,128]{3,2,1,0:T(8,128)(2,1)} %bitcast.98) | data formatting | bytes 25165824 | tf_op jit(solution)/shard_map/gather | solution.py:53
  204.3 16.0 %fusion.5 = f32[1,64,128,128]{2,3,1,0:T(8,128)} fusion(f32[64,64,128]{1,2,0:T(8,128)} %get-tuple-element.6, f32[64,64,128]{1,2,0:T(8,128)} %get-tuple-element.5, f32[64,128,128]{2,1,0:T(8,128)} %fusion.20, bf16[64,6,128,128]{3,2,1,0:T(8,128)(2,1)} %all-gather.2.cloned.1.call-done, bf16[64,6,128,128]{2,3,1,0:T(8,128)(2,1)} %copy.33, bf16[64,6]{1,0:T(8,128)(2,1)S(1)} %copy.32), kind=kOutput, calls=%fused_computation.18 | convolution fusion | flops 1620049920 | bytes 37749504 | tf_op jit(solution)/shard_map/bjvu,bjur->bvr/dot_general | solution.py:54
  220.3 5.6 %copy.37 = f32[1,64,128,128]{3,2,1,0:T(8,128)} copy(f32[1,64,128,128]{2,3,1,0:T(8,128)} %fusion.5) | data formatting | bytes 8388608 | tf_op jit(solution)/shard_map/broadcast_in_dim | solution.py:106
  (58 shorter events, 4.5 us)
Async XLA Ops:
  6.5 3.2 %copy-start = (bf16[8,512,128]{2,1,0:T(8,128)(2,1)S(1)}, bf16[8,512,128]{2,1,0:T(8,128)(2,1)}, u32[]{:S(2)}) copy-start(bf16[8,512,128]{2,1,0:T(8,128)(2,1)} %param.18) | copy-start | bytes 3145732
  6.5 0.8 copy-start.5
  6.5 197.7 %all-gather.2.cloned.1.call-start = ((), (), s32[]{:S(2)}) async-start(), calls=%async_computation.2 | async-start | bytes 18874368 | tf_op jit(solution)/shard_map/all_gather | solution.py:56
  12.0 113.7 %collective-permute-start.2 = (bf16[8,512,128]{1,2,0:T(8,128)(2,1)}, bf16[8,512,128]{1,2,0:T(8,128)(2,1)}, u32[]{:S(2)}, u32[]{:S(2)}) collective-permute-start(bf16[8,512,128]{1,2,0:T(8,128)(2,1)} %fusion.16), channel_id=1, source_target_pairs={{0,2},{2,4},{4,6},{6,8},{8,10},{10,12},{12,14},{14,16},{16,18},{18... | collective-permute-start | bytes 3145736 | tf_op jit(solution)/shard_map/ppermute | solution.py:12
  15.4 110.4 %collective-permute-start.3 = (bf16[8,512,128]{1,2,0:T(8,128)(2,1)}, bf16[8,512,128]{1,2,0:T(8,128)(2,1)}, u32[]{:S(2)}, u32[]{:S(2)}) collective-permute-start(bf16[8,512,128]{1,2,0:T(8,128)(2,1)} %fusion.16), channel_id=1, source_target_pairs={{2,0},{4,2},{6,4},{8,6},{10,8},{12,10},{14,12},{16,14},{18,16},{20... | collective-permute-start | bytes 3145736 | tf_op jit(solution)/shard_map/ppermute | solution.py:15
  16.7 151.0 %collective-permute-start = (bf16[1,64,128,128]{3,2,1,0:T(8,128)(2,1)}, bf16[1,64,128,128]{3,2,1,0:T(8,128)(2,1)}, u32[]{:S(2)}, u32[]{:S(2)}) collective-permute-start(bf16[1,64,128,128]{3,2,1,0:T(8,128)(2,1)} %param.13), channel_id=1, source_target_pairs={{0,2},{2,4},{4,6},{6,8},{8,10},{10,12},{12,14},{14,16},{16,18},{18... | collective-permute-start | bytes 6291464 | tf_op jit(solution)/shard_map/ppermute | solution.py:12
  22.3 145.3 %collective-permute-start.1 = (bf16[1,64,128,128]{3,2,1,0:T(8,128)(2,1)}, bf16[1,64,128,128]{3,2,1,0:T(8,128)(2,1)}, u32[]{:S(2)}, u32[]{:S(2)}) collective-permute-start(bf16[1,64,128,128]{3,2,1,0:T(8,128)(2,1)} %param.13), channel_id=1, source_target_pairs={{2,0},{4,2},{6,4},{8,6},{10,8},{12,10},{14,12},{16,14},{18,16},{20... | collective-permute-start | bytes 6291464 | tf_op jit(solution)/shard_map/ppermute | solution.py:15
  37.0 21.4 %copy-start.8 = (s32[8,16]{1,0:T(8,128)S(1)}, s32[8,16]{1,0:T(8,128)}, u32[]{:S(2)}) copy-start(s32[8,16]{1,0:T(8,128)} %param.21) | copy-start | bytes 1540
  37.0 21.5 %copy-start.10 = (s32[8,16]{1,0:T(8,128)S(1)}, s32[8,16]{1,0:T(8,128)}, u32[]{:S(2)}) copy-start(s32[8,16]{1,0:T(8,128)} %param.22) | copy-start | bytes 1540
  37.0 21.6 %copy-start.6 = (s32[16,32]{1,0:T(8,128)S(1)}, s32[16,32]{1,0:T(8,128)}, u32[]{:S(2)}) copy-start(s32[16,32]{1,0:T(8,128)} %param.24) | copy-start | bytes 6148
  37.0 21.7 %copy-start.9 = (s32[16,32]{1,0:T(8,128)S(1)}, s32[16,32]{1,0:T(8,128)}, u32[]{:S(2)}) copy-start(s32[16,32]{1,0:T(8,128)} %param.25) | copy-start | bytes 6148
  37.0 21.7 %copy-start.7 = (s32[64,6]{0,1:T(8,128)S(1)}, s32[64,6]{0,1:T(8,128)}, u32[]{:S(2)}) copy-start(s32[64,6]{0,1:T(8,128)} %param.16) | copy-start | bytes 4612
  37.0 22.0 %copy-start.11 = (f32[1,2]{1,0:T(1,128)S(1)}, f32[1,2]{1,0:T(1,128)}, u32[]{:S(2)}) copy-start(f32[1,2]{1,0:T(1,128)} %param.14) | copy-start | bytes 28
  49.9 15.8 %copy-start.2 = (f32[316,128]{1,0:T(8,128)S(1)}, f32[316,128]{1,0:T(8,128)}, u32[]{:S(2)}) copy-start(f32[316,128]{1,0:T(8,128)} %param.23) | copy-start | bytes 485380
  50.8 26.2 %all-to-all-start = ((bf16[16,2,8192]{2,1,0:T(2,128)(2,1)}), bf16[16,2,8192]{2,1,0:T(2,128)(2,1)}, u32[]{:S(2)}, u32[]{:S(2)}) async-start(bf16[16,2,8192]{2,1,0:T(2,128)(2,1)} %reshape.95), calls=%async_computation | async-start | bytes 1048576 | tf_op jit(solution)/shard_map/all_to_all | solution.py:77
  79.3 13.7 %copy-start.4 = (f32[16,128,32]{1,2,0:T(8,128)S(1)}, f32[16,128,32]{1,2,0:T(8,128)}, u32[]{:S(2)}) copy-start(f32[16,128,32]{1,2,0:T(8,128)} %multiply_bitcast_fusion) | copy-start | bytes 786436
  105.4 43.0 %all-to-all-start.1 = ((bf16[16,128,128]{1,2,0:T(8,128)(2,1)}), bf16[16,128,128]{1,2,0:T(8,128)(2,1)}, u32[]{:S(2)}, u32[]{:S(2)}) async-start(bf16[16,128,128]{1,2,0:T(8,128)(2,1)} %copy.54), calls=%async_computation.1 | async-start | bytes 1048576 | tf_op jit(solution)/shard_map/all_to_all | solution.py:83
  129.0 10.1 %copy-start.3 = (f32[8,512,16]{1,2,0:T(8,128)S(1)}, f32[8,512,16]{1,2,0:T(8,128)}, u32[]{:S(2)}) copy-start(f32[8,512,16]{1,2,0:T(8,128)} %multiply_bitcast_fusion.1) | copy-start | bytes 786436
  204.3 21.6 %copy-start.1 = (bf16[8,512,128]{2,1,0:T(8,128)(2,1)S(1)}, bf16[8,512,128]{2,1,0:T(8,128)(2,1)}, u32[]{:S(2)}) copy-start(bf16[8,512,128]{2,1,0:T(8,128)(2,1)} %param.18) | copy-start | bytes 3145732
Sparse Core Ops, SparseCore 0:
  8.9 155.2 all-gather.1
where the time goes:
time: 234 us; the launch traced here: 233 us
  local copies, waits for them, and re-layouts  78.6 us (34%)
  other arithmetic  51.2 us (22%)
  matrix products  49.1 us (21%)
  starting transfers between devices  39.5 us (17%)
  between operations  13.7 us (6%)
    gather x2, local copies, waits for them, and re-layouts, body(): near_source = haloed[local] * live_mask  30.6 us
    unnamed x4, other arithmetic  26.4 us
    gather x2, local copies, waits for them, and re-layouts, weighted_lists(): picked = pattern[local]  23.7 us
    all_to_all x1, starting transfers between devices, body(): lax.all_to_all(turned, 'box', split_axis=0, concat_axis=1, tiled=True)  20.4 us
    dot_general x1, matrix products, body(): jnp.einsum('bjvu,bjur->bvr', lax.all_gather(near_blocks, 'shift', axis=2,...  16 us
    dot_general x1, matrix products, body(): jnp.einsum('oqk,gokr->gqr', interp_two, upper.reshape(box_count // 64, 8,...  13.4 us
    dot_general x1, matrix products, body(): jnp.einsum('oqk,cqr->cokr', interp_one, local_in, preferred_element_type=...  10.8 us
    dot_general x1, other arithmetic, weighted_lists(): jnp.einsum('cjk,cjkr->ckr', weights, picked, preferred_element_type=jnp.f...  9.27 us
  transfers between devices with their start and end apart: 7, of which 0 were waited for; matrix products, arithmetic and copies ran while one was open for 67% of the time, Pallas kernels for 0%

commit v1 on v0

--- a/solution.py
+++ b/solution.py
@@ -80,7 +80,10 @@
         level2_source,
         0,
     ).astype(jnp.bfloat16)
-    incoming = lax.all_to_all(turned, "box", split_axis=0, concat_axis=1, tiled=True)
+    incoming = jnp.concatenate(
+        lax.all_to_all(jnp.stack(jnp.split(turned, lax.axis_size("box"), axis=0)), "box", 0, 0),
+        axis=1,
+    )
     parents = box_count // 8
     upper_rim = extended(upper, (("box", 0),), parents)
     across = weighted_lists(

time: 234 us -> 243 us (1.038)
  matrix products: 49.1 us -> 64.1 us
  other arithmetic: 51.2 us -> 37.5 us
  local copies, waits for them, and re-layouts: 78.6 us -> 84.3 us
  starting transfers between devices: 39.5 us -> 42.3 us
    dot_general x0 -> x1, matrix products: none -> 16.8 us  [weighted_lists(): jnp.einsum('cjk,cjkr->ckr', weights, picked, preferred_element_type=jnp.f...]
    unnamed x4 -> x2, other arithmetic: 26.4 us -> 12.6 us
    unnamed x29 -> x42, local copies, waits for them, and re-layouts: 7.13 us -> 16.1 us
  transfers between devices with their start and end apart: 7 -> 7, of which waited for: 0 -> 0; matrix products, arithmetic and copies ran while one was open for 67% -> 66% of each run, Pallas kernels for 0% -> 0%
where the time goes in v1:
time: 243 us; the launch traced here: 242 us
  local copies, waits for them, and re-layouts  84.3 us (35%)
  matrix products  64.1 us (26%)
  starting transfers between devices  42.3 us (17%)
  other arithmetic  37.5 us (15%)
  between operations  13.7 us (6%)
    gather x2, local copies, waits for them, and re-layouts, body(): near_source = haloed[local] * live_mask  30.6 us
    gather x2, local copies, waits for them, and re-layouts, weighted_lists(): picked = pattern[local]  23.7 us
    all_to_all x1, starting transfers between devices, body(): lax.all_to_all(jnp.stack(jnp.split(turned, lax.axis_size('box'), axis=0))...  22.8 us
    dot_general x1, matrix products, weighted_lists(): jnp.einsum('cjk,cjkr->ckr', weights, picked, preferred_element_type=jnp.f...  16.8 us
    unnamed x42, local copies, waits for them, and re-layouts  16.1 us
    dot_general x1, matrix products, body(): jnp.einsum('bjvu,bjur->bvr', lax.all_gather(near_blocks, 'shift', axis=2,...  16 us
    unnamed x2, other arithmetic  12.6 us
    dot_general x1, matrix products, body(): jnp.einsum('oqk,gokr->gqr', interp_two, upper.reshape(box_count // 64, 8,...  11.5 us
  transfers between devices with their start and end apart: 7, of which 0 were waited for; matrix products, arithmetic and copies ran while one was open for 66% of the time, Pallas kernels for 0%

profile of v1, /device:TPU:0, one launch (start us, length us, event | category | flops | bytes accessed | tf_op | source)
XLA Modules:
  0.0 241.9 jit_solution(10915034410267981283)
XLA Ops:
  6.5 2.4 %fusion.15 = bf16[64,128,128]{2,1,0:T(8,128)(2,1)S(1)} fusion(bf16[1,64,128,128]{3,2,1,0:T(8,128)(2,1)} %param.13, bf16[128,128]{1,0:T(8,128)(2,1)} %param.17), kind=kOutput, calls=%fused_computation.30 | convolution fusion | flops 269484032 | bytes 4227072 | tf_op jit(solution)/shard_map/ku,bur->bkr/dot_general | solution.py:61
  9.0 2.3 fusion.18
  11.3 3.4 %collective-permute-start.2 = (bf16[8,512,128]{1,2,0:T(8,128)(2,1)}, bf16[8,512,128]{1,2,0:T(8,128)(2,1)}, u32[]{:S(2)}, u32[]{:S(2)}) collective-permute-start(bf16[8,512,128]{1,2,0:T(8,128)(2,1)} %fusion.18), channel_id=1, source_target_pairs={{0,2},{2,4},{4,6},{6,8},{8,10},{10,12},{12,14},{14,16},{16,18},{18... | collective-permute-start | bytes 3145736 | tf_op jit(solution)/shard_map/ppermute | solution.py:12
  14.6 1.3 collective-permute-start.3
  15.9 5.5 %collective-permute-start = (bf16[1,64,128,128]{3,2,1,0:T(8,128)(2,1)}, bf16[1,64,128,128]{3,2,1,0:T(8,128)(2,1)}, u32[]{:S(2)}, u32[]{:S(2)}) collective-permute-start(bf16[1,64,128,128]{3,2,1,0:T(8,128)(2,1)} %param.13), channel_id=1, source_target_pairs={{0,2},{2,4},{4,6},{6,8},{8,10},{10,12},{12,14},{14,16},{16,18},{18... | collective-permute-start | bytes 6291464 | tf_op jit(solution)/shard_map/ppermute | solution.py:12
  21.4 1.3 collective-permute-start.1
  22.7 11.5 %fusion.9 = bf16[1,2048,128]{1,2,0:T(8,128)(2,1)S(1)} fusion(bf16[8,512,128]{1,2,0:T(8,128)(2,1)} %fusion.18, bf16[8,2048,512]{2,1,0:T(8,128)(2,1)} %param.19), kind=kOutput, calls=%fused_computation.24 | convolution fusion | flops 2147745792 | bytes 18350080 | tf_op jit(solution)/shard_map/oqk,gokr->gqr/dot_general | solution.py:70
  34.3 0.8 copy.51
  35.6 11.5 %reduce.2 = bf16[2048,128]{1,0:T(8,128)(2,1)S(1)} reduce(bf16[2048,1,128]{2,1,0:T(2,128)(2,1)S(1)} %bitcast.169, bf16[]{:T(256)} %broadcast.52), dimensions={1}, to_apply=%bitcast.153.reduce_sub_computation | reduce | bytes 1048578
  47.1 0.9 reshape.92
  48.1 8.1 %all-to-all-start = ((bf16[16,2,8192]{2,1,0:T(2,128)(2,1)}), bf16[16,2,8192]{2,1,0:T(2,128)(2,1)}, u32[]{:S(2)}, u32[]{:S(2)}) async-start(bf16[16,2,8192]{2,1,0:T(2,128)(2,1)} %reshape.92), calls=%async_computation | async-start | bytes 1048576 | tf_op jit(solution)/shard_map/all_to_all | solution.py:77
  56.8 1.0 gather_fusion.3
  57.9 0.7 fusion.43
  58.7 3.2 %copy.50 = bf16[1,64,128,128]{2,3,1,0:T(8,128)(2,1)S(1)} copy(bf16[1,64,128,128]{3,2,1,0:T(8,128)(2,1)} %param.13) | data formatting | bytes 4194304 | tf_op args[0]
  62.0 2.0 copy.63
  64.0 2.7 %gather_fusion.1 = f32[128,512]{1,0:T(8,128)} fusion(f32[316,512]{1,0:T(8,128)} %param.20, s32[1024]{0:T(1024)S(1)} %pad_clamp_fusion.3), kind=kCustom, calls=%fused_computation.1 | custom fusion | bytes 524800 | tf_op jit(solution)/shard_map/gather | solution.py:23
  66.7 1.0 multiply_bitcast_fusion.1
  67.7 6.1 %fusion.5 = (f32[64,64,128]{1,2,0:T(8,128)}, f32[64,64,128]{1,2,0:T(8,128)}) fusion(f32[]{:T(128)} %bitcast.52, f32[]{:T(128)} %bitcast.51, bf16[64,128,128]{1,2,0:T(8,128)(2,1)S(1)} %bitcast.165), kind=kLoop, calls=%fused_computation.16 | loop fusion | flops 4194304 | bytes 6291464 | tf_op jit(solution)/shard_map/sub | solution.py:107
  73.9 2.2 reshape.93
  76.2 13.6 %gather_fusion.4 = bf16[512,128,128]{2,1,0:T(8,128)(2,1)} fusion(bf16[16,128,128]{2,1,0:T(8,128)(2,1)S(1)} %bitcast.163, s32[1024]{0:T(1024)S(1)} %get-tuple-element.9), kind=kCustom, calls=%fused_computation.4 | custom fusion | bytes 33556480 | tf_op jit(solution)/shard_map/gather | solution.py:24
  89.8 16.8 %fusion = f32[16,128,1,128]{3,2,1,0:T(1,128)S(1)} fusion(bf16[16,32,128,1]{1,3,2,0:T(2,128)(2,1)S(1)} %copy-done.3, bf16[16,32,128,128]{3,2,1,0:T(8,128)(2,1)} %bitcast.166), kind=kOutput, calls=%fused_computation.6 | convolution fusion | flops 16777216 | bytes 17956864 | tf_op jit(solution)/shard_map/cjk,cjkr->ckr/dot_general | solution.py:25
  116.4 22.8 %all-to-all-start.1 = ((bf16[16,1,128,128]{3,2,1,0:T(8,128)(2,1)}), bf16[16,1,128,128]{3,2,1,0:T(8,128)(2,1)}, u32[]{:S(2)}, u32[]{:S(2)}) async-start(bf16[16,1,128,128]{3,2,1,0:T(8,128)(2,1)} %fusion.22), calls=%async_computation.1 | async-start | bytes 1048576 | tf_op jit(solution)/shard_map/all_to_all | solution.py:84
  139.2 3.2 %pad_maximum_fusion = bf16[24,512,128]{1,2,0:T(8,128)(2,1)} fusion(bf16[8,512,128]{1,2,0:T(8,128)(2,1)} %collective-permute-done.3, bf16[8,512,128]{1,2,0:T(8,128)(2,1)} %fusion.18, bf16[8,512,128]{1,2,0:T(8,128)(2,1)} %collective-permute-done.2), kind=kLoop, calls=%fused_computation.21 | loop fusion | flops 3145728 | bytes 6291456 | tf_op jit(solution)/shard_map/concatenate | solution.py:16
  142.4 10.0 %gather_fusion.2 = bf16[128,512,128]{1,2,0:T(8,128)(2,1)} fusion(bf16[24,512,128]{1,2,0:T(8,128)(2,1)} %pad_maximum_fusion, s32[1024]{0:T(1024)S(1)} %pad_clamp_fusion.2), kind=kCustom, calls=%fused_computation.2 | custom fusion | bytes 33554944 | tf_op jit(solution)/shard_map/gather | solution.py:24
  152.5 9.3 %multiply_reduce_fusion = f32[8,512,128]{1,2,0:T(8,128)S(1)} fusion(f32[8,512,16]{1,2,0:T(8,128)S(1)} %multiply_bitcast_fusion.1, bf16[128,512,128]{1,2,0:T(8,128)(2,1)} %gather_fusion.2), kind=kLoop, calls=%fused_computation.5 | loop fusion | flops 24641536 | bytes 19136512 | tf_op jit(solution)/shard_map/cjk,cjkr->ckr/dot_general | solution.py:25
  161.8 10.8 %convolution_convert_fusion = bf16[8,128,8,128]{3,1,2,0:T(8,128)(2,1)} fusion(bf16[8,512,128]{2,1,0:T(8,128)(2,1)S(1)} %copy-done, f32[8,512,128]{1,2,0:T(8,128)S(1)} %multiply_reduce_fusion, bf16[2048,128,1]{1,0,2:T(8,128)(2,1)} %bitcast.62, bf16[8,2048,512]{2,1,0:T(8,128)(2,1)} %param.19), kind=kOutput, calls=%fused_computation.31 | convolution fusion | flops 3223322624 | bytes 22544384 | tf_op jit(solution)/shard_map/oqk,cqr->cokr/dot_general | solution.py:97
  172.6 4.2 %fusion.38 = f32[64,128,128]{2,1,0:T(8,128)} fusion(bf16[64,128,128]{1,2,0:T(8,128)(2,1)} %bitcast.167, bf16[128,128]{1,0:T(8,128)(2,1)S(1)} %copy-done.4), kind=kOutput, calls=%fused_computation.70 | convolution fusion | flops 268435456 | bytes 6324224 | tf_op jit(solution)/shard_map/ku,bkr->bur/dot_general | solution.py:101
  176.8 6.0 %maximum_bitcast_fusion = bf16[192,128,128]{2,1,0:T(8,128)(2,1)} fusion(bf16[1,64,128,128]{3,2,1,0:T(8,128)(2,1)} %collective-permute-done.1, bf16[1,64,128,128]{3,2,1,0:T(8,128)(2,1)} %param.13, bf16[1,64,128,128]{3,2,1,0:T(8,128)(2,1)} %collective-permute-done), kind=kLoop, calls=%fused_computation.10 | loop fusion | flops 6291456 | bytes 12582912 | tf_op jit(solution)/shard_map/squeeze | solution.py:52
  182.8 13.9 %gather_fusion = bf16[384,128,128]{2,1,0:T(8,128)(2,1)} fusion(bf16[192,128,128]{2,1,0:T(8,128)(2,1)} %maximum_bitcast_fusion, s32[1024]{0:T(1024)S(1)} %pad_clamp_fusion.4), kind=kCustom, calls=%fused_computation | custom fusion | bytes 25167360 | tf_op jit(solution)/shard_map/gather | solution.py:53
  196.8 16.6 %copy.49 = bf16[64,6,128,128]{2,3,1,0:T(8,128)(2,1)} copy(bf16[64,6,128,128]{3,2,1,0:T(8,128)(2,1)} %bitcast.164) | data formatting | bytes 25165824 | tf_op jit(solution)/shard_map/gather | solution.py:53
  213.4 16.0 %fusion.7 = f32[1,64,128,128]{2,3,1,0:T(8,128)} fusion(f32[64,64,128]{1,2,0:T(8,128)} %get-tuple-element.6, f32[64,64,128]{1,2,0:T(8,128)} %get-tuple-element.5, f32[64,128,128]{2,1,0:T(8,128)} %fusion.38, bf16[64,6,128,128]{3,2,1,0:T(8,128)(2,1)} %all-gather.2.cloned.1.call-done, bf16[64,6,128,128]{2,3,1,0:T(8,128)(2,1)} %copy.49, bf16[64,6]{1,0:T(8,128)(2,1)S(1)} %copy.48), kind=kOutput, calls=%fused_computation.19 | convolution fusion | flops 1620049920 | bytes 37749504 | tf_op jit(solution)/shard_map/bjvu,bjur->bvr/dot_general | solution.py:54
  229.4 5.6 %copy.53 = f32[1,64,128,128]{3,2,1,0:T(8,128)} copy(f32[1,64,128,128]{2,3,1,0:T(8,128)} %fusion.7) | data formatting | bytes 8388608 | tf_op jit(solution)/shard_map/broadcast_in_dim | solution.py:109
  (70 shorter events, 11.3 us)
Async XLA Ops:
  6.5 2.4 %copy-start = (bf16[8,512,128]{2,1,0:T(8,128)(2,1)S(1)}, bf16[8,512,128]{2,1,0:T(8,128)(2,1)}, u32[]{:S(2)}) copy-start(bf16[8,512,128]{2,1,0:T(8,128)(2,1)} %param.18) | copy-start | bytes 3145732
  6.5 206.9 %all-gather.2.cloned.1.call-start = ((), (), s32[]{:S(2)}) async-start(), calls=%async_computation.2 | async-start | bytes 18874368 | tf_op jit(solution)/shard_map/all_gather | solution.py:56
  11.3 127.9 %collective-permute-start.2 = (bf16[8,512,128]{1,2,0:T(8,128)(2,1)}, bf16[8,512,128]{1,2,0:T(8,128)(2,1)}, u32[]{:S(2)}, u32[]{:S(2)}) collective-permute-start(bf16[8,512,128]{1,2,0:T(8,128)(2,1)} %fusion.18), channel_id=1, source_target_pairs={{0,2},{2,4},{4,6},{6,8},{8,10},{10,12},{12,14},{14,16},{16,18},{18... | collective-permute-start | bytes 3145736 | tf_op jit(solution)/shard_map/ppermute | solution.py:12
  14.6 124.6 %collective-permute-start.3 = (bf16[8,512,128]{1,2,0:T(8,128)(2,1)}, bf16[8,512,128]{1,2,0:T(8,128)(2,1)}, u32[]{:S(2)}, u32[]{:S(2)}) collective-permute-start(bf16[8,512,128]{1,2,0:T(8,128)(2,1)} %fusion.18), channel_id=1, source_target_pairs={{2,0},{4,2},{6,4},{8,6},{10,8},{12,10},{14,12},{16,14},{18,16},{20... | collective-permute-start | bytes 3145736 | tf_op jit(solution)/shard_map/ppermute | solution.py:15
  15.9 160.9 %collective-permute-start = (bf16[1,64,128,128]{3,2,1,0:T(8,128)(2,1)}, bf16[1,64,128,128]{3,2,1,0:T(8,128)(2,1)}, u32[]{:S(2)}, u32[]{:S(2)}) collective-permute-start(bf16[1,64,128,128]{3,2,1,0:T(8,128)(2,1)} %param.13), channel_id=1, source_target_pairs={{0,2},{2,4},{4,6},{6,8},{8,10},{10,12},{12,14},{14,16},{16,18},{18... | collective-permute-start | bytes 6291464 | tf_op jit(solution)/shard_map/ppermute | solution.py:12
  21.4 155.4 %collective-permute-start.1 = (bf16[1,64,128,128]{3,2,1,0:T(8,128)(2,1)}, bf16[1,64,128,128]{3,2,1,0:T(8,128)(2,1)}, u32[]{:S(2)}, u32[]{:S(2)}) collective-permute-start(bf16[1,64,128,128]{3,2,1,0:T(8,128)(2,1)} %param.13), channel_id=1, source_target_pairs={{2,0},{4,2},{6,4},{8,6},{10,8},{12,10},{14,12},{16,14},{18,16},{20... | collective-permute-start | bytes 6291464 | tf_op jit(solution)/shard_map/ppermute | solution.py:15
  34.2 22.0 %copy-start.8 = (s32[16,32]{1,0:T(8,128)S(1)}, s32[16,32]{1,0:T(8,128)}, u32[]{:S(2)}) copy-start(s32[16,32]{1,0:T(8,128)} %param.25) | copy-start | bytes 6148
  34.2 22.0 %copy-start.5 = (s32[16,32]{1,0:T(8,128)S(1)}, s32[16,32]{1,0:T(8,128)}, u32[]{:S(2)}) copy-start(s32[16,32]{1,0:T(8,128)} %param.24) | copy-start | bytes 6148
  34.2 22.1 %copy-start.7 = (s32[8,16]{1,0:T(8,128)S(1)}, s32[8,16]{1,0:T(8,128)}, u32[]{:S(2)}) copy-start(s32[8,16]{1,0:T(8,128)} %param.21) | copy-start | bytes 1540
  34.3 22.2 %copy-start.9 = (s32[8,16]{1,0:T(8,128)S(1)}, s32[8,16]{1,0:T(8,128)}, u32[]{:S(2)}) copy-start(s32[8,16]{1,0:T(8,128)} %param.22) | copy-start | bytes 1540
  34.3 22.3 %copy-start.6 = (s32[64,6]{0,1:T(8,128)S(1)}, s32[64,6]{0,1:T(8,128)}, u32[]{:S(2)}) copy-start(s32[64,6]{0,1:T(8,128)} %param.16) | copy-start | bytes 4612
  34.3 22.5 %copy-start.2 = (f32[316,128]{1,0:T(8,128)S(1)}, f32[316,128]{1,0:T(8,128)}, u32[]{:S(2)}) copy-start(f32[316,128]{1,0:T(8,128)} %param.23) | copy-start | bytes 485380
  34.3 23.6 %copy-start.10 = (f32[1,2]{1,0:T(1,128)S(1)}, f32[1,2]{1,0:T(1,128)}, u32[]{:S(2)}) copy-start(f32[1,2]{1,0:T(1,128)} %param.14) | copy-start | bytes 28
  48.1 25.8 %all-to-all-start = ((bf16[16,2,8192]{2,1,0:T(2,128)(2,1)}), bf16[16,2,8192]{2,1,0:T(2,128)(2,1)}, u32[]{:S(2)}, u32[]{:S(2)}) async-start(bf16[16,2,8192]{2,1,0:T(2,128)(2,1)} %reshape.92), calls=%async_computation | async-start | bytes 1048576 | tf_op jit(solution)/shard_map/all_to_all | solution.py:77
  76.2 13.6 %copy-start.3 = (bf16[16,32,128,1]{1,3,2,0:T(2,128)(2,1)S(1)}, bf16[16,32,128,1]{1,3,2,0:T(2,128)(2,1)}, u32[]{:S(2)}) copy-start(bf16[16,32,128,1]{1,3,2,0:T(2,128)(2,1)} %copy.63) | copy-start | bytes 393220
  116.4 45.3 %all-to-all-start.1 = ((bf16[16,1,128,128]{3,2,1,0:T(8,128)(2,1)}), bf16[16,1,128,128]{3,2,1,0:T(8,128)(2,1)}, u32[]{:S(2)}, u32[]{:S(2)}) async-start(bf16[16,1,128,128]{3,2,1,0:T(8,128)(2,1)} %fusion.22), calls=%async_computation.1 | async-start | bytes 1048576 | tf_op jit(solution)/shard_map/all_to_all | solution.py:84
  161.8 10.8 %copy-start.4 = (bf16[128,128]{1,0:T(8,128)(2,1)S(1)}, bf16[128,128]{1,0:T(8,128)(2,1)}, u32[]{:S(2)}) copy-start(bf16[128,128]{1,0:T(8,128)(2,1)} %param.17) | copy-start | bytes 98308
  213.4 21.6 %copy-start.1 = (bf16[8,512,128]{2,1,0:T(8,128)(2,1)S(1)}, bf16[8,512,128]{2,1,0:T(8,128)(2,1)}, u32[]{:S(2)}) copy-start(bf16[8,512,128]{2,1,0:T(8,128)(2,1)} %param.18) | copy-start | bytes 3145732
Sparse Core Ops, SparseCore 0:
  22.9 155.8 all-gather.1
